TPU v7x, 32 devices: a whole 2x2x4 slice. The times are simulated.
32 devices in a mesh: row: 4 (over y, core), col: 8 (over z, x).
Axes of the slice: x: 2, y: 2, z: 4, core: 2. Of those that a mesh axis runs over, the one named last changes fastest.
Arguments:
- diag_block: float32 [1024, 1024], P('row')
- panel: bfloat16 [16, 1024, 1024], P('col', 'row'), may hold values from -1 to 1
- trailing: bfloat16 [8, 12, 1024, 1024], P('col', None, 'row'), may hold values from -6 to 6
- slot_rows: int32 [8, 12], replicated, may hold values from -1 to 15, as said below
- slot_cols: int32 [8, 12], replicated, may hold values from 0 to 1, as said below
Outputs:
- panel_factor: bfloat16 [16, 1024, 1024], P('col', 'row')
- updated: bfloat16 [8, 12, 1024, 1024], P('col', None, 'row')
Inputs may be any that keep to these rules, and one draw needn't show every extreme that they name: Slot s of grid column c holds the tile at tile row slot_rows[c, s] and tile column 2 * c + slot_cols[c, s] of the trailing matrix, or nothing where slot_rows[c, s] is -1. Live slots come first in each column; the pairs of one column are distinct and lie on or below the diagonal (tile row at least tile column). Within one grid column, live slots whose tile rows a and a' have a // 2 == a' // 2 have a == a'. Every column holds at least one live slot, column 0 fills all 12 slots and column 4 holds exactly one. `slot_cols`: 0 in empty slots.
All inputs are finite; a program needn't handle non-finite values.
Results may differ from a plain program's by a relative error of at most 0.0019.
Values may be sent and summed in bfloat16 or wider, within the bound.
A program may use at most 128 MiB of HBM per device.

v0:
```python
import jax
import jax.numpy as jnp
from jax import lax
from jax.sharding import PartitionSpec as P


def slot_product(slices, left_ids, source_tiles, col_ids, position):
    left_slice = lax.dynamic_index_in_dim(slices, left_ids[position], 0, keepdims=False)
    right_tile = lax.dynamic_index_in_dim(source_tiles, col_ids[position], 0, keepdims=False)
    return lax.dot_general(
        left_slice, right_tile, (((1,), (1,)), ((), ())), preferred_element_type=jnp.float32
    )


def subtract_slot(buffer, position, update):
    previous = lax.dynamic_index_in_dim(buffer, position, 0, keepdims=False).astype(jnp.float32)
    return lax.dynamic_update_index_in_dim(
        buffer, (previous - update).astype(jnp.bfloat16), position, 0
    )


def local(diag_block, panel, trailing, slot_rows, slot_cols):
    diag_full = lax.all_gather(diag_block, "row", axis=0, tiled=True)
    factor = jnp.linalg.cholesky(diag_full)
    tile_count, row_count, tile_width = panel.shape
    stacked = panel.astype(jnp.float32).reshape(tile_count * row_count, tile_width)
    solved = lax.linalg.triangular_solve(factor, stacked.T, left_side=True, lower=True)
    panel_factor = solved.T.reshape(tile_count, row_count, tile_width).astype(jnp.bfloat16)
    whole_tiles = lax.all_gather(panel_factor, "row", axis=1, tiled=True)
    column_index = lax.axis_index("col")
    own_rows = lax.dynamic_index_in_dim(slot_rows, column_index, 0, keepdims=False)
    own_cols = lax.dynamic_index_in_dim(slot_cols, column_index, 0, keepdims=False)
    own_count = jnp.sum((own_rows >= 0).astype(jnp.int32))
    mine = (slot_rows >= 0) & (slot_rows // tile_count == column_index)
    local_pick = jnp.max(jnp.where(mine, slot_rows % tile_count, 0), axis=1)
    wanted = jnp.any(mine, axis=1)
    picks = jnp.arange(tile_count, dtype=jnp.int32)
    selector = ((local_pick[:, None] == picks[None, :]) & wanted[:, None]).astype(jnp.bfloat16)
    outgoing = jnp.einsum(
        "dp,prt->drt", selector, panel_factor, preferred_element_type=jnp.float32
    ).astype(jnp.bfloat16)
    slices = lax.all_to_all(outgoing, "col", split_axis=0, concat_axis=0, tiled=True)
    left_ids = own_rows // tile_count

    def own_step(position, buffer):
        return subtract_slot(
            buffer, position, slot_product(slices, left_ids, whole_tiles, own_cols, position)
        )

    buffer = lax.fori_loop(0, own_count, own_step, trailing[0])
    return (panel_factor, buffer[None])


def solution(mesh):
    return jax.shard_map(
        local,
        mesh=mesh,
        in_specs=(P("row", None), P("col", "row", None), P("col", None, "row", None), P(), P()),
        out_specs=(P("col", "row", None), P("col", None, "row", None)),
        check_vma=False,
    )
```

profile of v0, /device:TPU:0, one launch (start us, length us, event | category | flops | bytes accessed | tf_op | source)
XLA Modules:
  0.0 636.3 jit_solution(12007265828174726082)
XLA Ops:
  7.3 6.3 copy.70
  15.5 36.7 %all-gather.3.cloned.1.call-done = f32[1024,1024]{0,1:T(8,128)} async-done(((f32[256,1024]{0,1:T(8,128)}), f32[1024,1024]{0,1:T(8,128)}) %all-gather.3.cloned.1.call-update) | async-done | bytes 4194320 | tf_op jit(solution)/shard_map/all_gather | solution.py:23
  52.3 5.3 copy.14
  57.6 4.4 fusion.18
  62.0 1.9 copy-done.1
  64.0 11.7 %cholesky.223 = f32[128,128]{1,0:T(8,128)S(1)} custom-call(f32[128,128]{1,0:T(8,128)S(1)} %cholesky.580), custom_call_target="Cholesky" | custom-call | tf_op jit(solution)/shard_map/jit(cholesky)/cholesky | solution.py:24
  75.7 9.8 %custom-call.62 = f32[1,128,128]{1,2,0:T(8,128)S(1)} custom-call(f32[1,128,128]{2,1,0:T(8,128)S(1)} %get-tuple-element.124), custom_call_target="InvertDiagBlocksLowerTriangular" | custom-call | tf_op jit(solution)/shard_map/jit(cholesky)/cholesky | solution.py:24
  85.5 2.5 cholesky.255
  88.0 2.4 constant_dynamic-update-slice_fusion.24
  92.0 12.0 %cholesky.244 = f32[128,128]{1,0:T(8,128)S(1)} custom-call(f32[128,128]{1,0:T(8,128)S(1)} %cholesky.584), custom_call_target="Cholesky" | custom-call | tf_op jit(solution)/shard_map/jit(cholesky)/cholesky | solution.py:24
  104.7 9.8 %custom-call.63 = f32[1,128,128]{1,2,0:T(8,128)S(1)} custom-call(f32[1,128,128]{2,1,0:T(8,128)S(1)} %get-tuple-element.121), custom_call_target="InvertDiagBlocksLowerTriangular" | custom-call | tf_op jit(solution)/shard_map/jit(cholesky)/cholesky | solution.py:24
  115.7 2.1 convolution_subtract_fusion.1
  117.8 11.7 %cholesky.468 = f32[128,128]{1,0:T(8,128)S(1)} custom-call(f32[128,128]{1,0:T(8,128)S(1)} %cholesky.589), custom_call_target="Cholesky" | custom-call | tf_op jit(solution)/shard_map/jit(cholesky)/cholesky | solution.py:24
  130.9 9.8 %custom-call.64 = f32[1,128,128]{1,2,0:T(8,128)S(1)} custom-call(f32[1,128,128]{2,1,0:T(8,128)S(1)} %get-tuple-element.118), custom_call_target="InvertDiagBlocksLowerTriangular" | custom-call | tf_op jit(solution)/shard_map/jit(cholesky)/cholesky | solution.py:24
  141.8 2.4 convolution_subtract_fusion.2
  144.2 11.8 %cholesky.487 = f32[128,128]{1,0:T(8,128)S(1)} custom-call(f32[128,128]{1,0:T(8,128)S(1)} %cholesky.594), custom_call_target="Cholesky" | custom-call | tf_op jit(solution)/shard_map/jit(cholesky)/cholesky | solution.py:24
  157.4 9.8 %custom-call.65 = f32[1,128,128]{1,2,0:T(8,128)S(1)} custom-call(f32[1,128,128]{2,1,0:T(8,128)S(1)} %get-tuple-element.115), custom_call_target="InvertDiagBlocksLowerTriangular" | custom-call | tf_op jit(solution)/shard_map/jit(cholesky)/cholesky | solution.py:24
  168.3 2.3 convolution_subtract_fusion.10
  170.6 11.7 %cholesky.506 = f32[128,128]{1,0:T(8,128)S(1)} custom-call(f32[128,128]{1,0:T(8,128)S(1)} %cholesky.599), custom_call_target="Cholesky" | custom-call | tf_op jit(solution)/shard_map/jit(cholesky)/cholesky | solution.py:24
  183.7 10.0 %custom-call.66 = f32[1,128,128]{1,2,0:T(8,128)S(1)} custom-call(f32[1,128,128]{2,1,0:T(8,128)S(1)} %get-tuple-element.112), custom_call_target="InvertDiagBlocksLowerTriangular" | custom-call | tf_op jit(solution)/shard_map/jit(cholesky)/cholesky | solution.py:24
  194.7 2.3 convolution_subtract_fusion.11
  197.0 11.7 %cholesky.526 = f32[128,128]{1,0:T(8,128)S(1)} custom-call(f32[128,128]{1,0:T(8,128)S(1)} %cholesky.604), custom_call_target="Cholesky" | custom-call | tf_op jit(solution)/shard_map/jit(cholesky)/cholesky | solution.py:24
  210.0 9.8 %custom-call.67 = f32[1,128,128]{1,2,0:T(8,128)S(1)} custom-call(f32[1,128,128]{2,1,0:T(8,128)S(1)} %get-tuple-element.109), custom_call_target="InvertDiagBlocksLowerTriangular" | custom-call | tf_op jit(solution)/shard_map/jit(cholesky)/cholesky | solution.py:24
  220.7 2.0 convolution_subtract_fusion.12
  222.8 12.1 %cholesky.546 = f32[128,128]{1,0:T(8,128)S(1)} custom-call(f32[128,128]{1,0:T(8,128)S(1)} %cholesky.609), custom_call_target="Cholesky" | custom-call | tf_op jit(solution)/shard_map/jit(cholesky)/cholesky | solution.py:24
  236.1 9.8 %custom-call.68 = f32[1,128,128]{1,2,0:T(8,128)S(1)} custom-call(f32[1,128,128]{2,1,0:T(8,128)S(1)} %get-tuple-element.106), custom_call_target="InvertDiagBlocksLowerTriangular" | custom-call | tf_op jit(solution)/shard_map/jit(cholesky)/cholesky | solution.py:24
  246.8 1.8 convolution_subtract_fusion.13
  248.6 11.7 %cholesky.564 = f32[128,128]{1,0:T(8,128)S(1)} custom-call(f32[128,128]{1,0:T(8,128)S(1)} %convolution_subtract_fusion.13), custom_call_target="Cholesky" | custom-call | tf_op jit(solution)/shard_map/jit(cholesky)/cholesky | solution.py:24
  267.2 4.8 select_select_fusion
  272.0 27.8 %while.12 = (s32[]{:T(128)}, f32[1024,1024]{1,0:T(8,128)}, s32[8,2]{0,1:T(2,128)S(1)}, f32[8,128,128]{2,1,0:T(8,128)}, s32[]{:T(128)}) while((s32[]{:T(128)}, f32[1024,1024]{1,0:T(8,128)}, s32[8,2]{0,1:T(2,128)S(1)}, f32[8,128,128]{2,1,0:T(8,128)}, s32[]{:T(128)}) %tuple.75), condition=%wide.while_cond, body=%wide.while_body.sunk | while | flops 2 | bytes 132205 | solution.py:27
  272.6 2.9 bitcast_dynamic-update-slice_fusion.2
  276.1 2.9 bitcast_dynamic-update-slice_fusion.2
  279.6 2.9 bitcast_dynamic-update-slice_fusion.2
  283.0 2.9 bitcast_dynamic-update-slice_fusion.2
  286.5 2.9 bitcast_dynamic-update-slice_fusion.2
  290.0 2.9 bitcast_dynamic-update-slice_fusion.2
  293.5 2.9 bitcast_dynamic-update-slice_fusion.2
  297.0 2.8 bitcast_dynamic-update-slice_fusion.2
  299.8 80.2 %custom-call.69 = f32[8,128,128]{1,2,0:T(8,128)} custom-call(f32[8,128,128]{2,1,0:T(8,128)} %get-tuple-element.48), custom_call_target="InvertDiagBlocksLowerTriangular" | custom-call | tf_op jit(solution)/shard_map/triangular_solve | solution.py:27
  384.1 1.9 convolution_subtract_fusion.5
  386.5 2.4 convolution_subtract_fusion.8
  389.3 2.8 convolution_subtract_fusion.9
  392.9 3.3 convolution_subtract_fusion.4
  396.7 3.6 convolution_subtract_fusion.7
  400.8 4.4 convolution_subtract_fusion.3
  405.9 2.5 copy.15
  410.2 4.3 copy.16
  414.5 5.5 all-to-all-start
  420.1 2.5 copy.18
  423.3 34.7 %all-gather.5.cloned.1.call-done = bf16[2,1024,1024]{2,1,0:T(8,128)(2,1)} async-done(((bf16[2,256,1024]{2,1,0:T(8,128)(2,1)}), bf16[2,1024,1024]{2,1,0:T(8,128)(2,1)}) %all-gather.5.cloned.1.call-update) | async-done | bytes 4194320 | tf_op jit(solution)/shard_map/all_gather | solution.py:29
  458.0 55.8 %all-to-all-done = bf16[8,256,1024]{2,1,0:T(8,128)(2,1)} async-done(((bf16[8,256,1024]{2,1,0:T(8,128)(2,1)}), bf16[8,256,1024]{2,1,0:T(8,128)(2,1)}, u32[]{:S(2)}, u32[]{:S(2)}) %all-to-all-start) | async-done | bytes 4194336 | tf_op jit(solution)/shard_map/all_to_all | solution.py:42
  513.8 115.5 %while.11 = (s32[]{:T(128)}, bf16[12,256,1024]{2,1,0:T(8,128)(2,1)}, s32[]{:T(128)}, s32[12]{0:T(128)S(1)}, bf16[8,256,1024]{2,1,0:T(8,128)(2,1)}, /*index=5*/s3...) while((s32[]{:T(128)}, ...), condition=%wide.region_20.21_spmd, body=%wide.region_19.20_spmd.sunk | while | flops 537657344 | bytes 4718859 | solution.py:50
  520.0 3.3 fusion.114
  529.6 3.3 fusion.114
  539.2 3.3 fusion.114
  548.7 3.3 fusion.114
  558.3 3.3 fusion.114
  567.9 3.3 fusion.114
  577.5 3.3 fusion.114
  587.0 3.3 fusion.114
  596.6 3.3 fusion.114
  606.2 3.3 fusion.114
  615.8 3.3 fusion.114
  625.3 3.3 fusion.114
  (123 shorter events, 60.0 us)
Async XLA Ops:
  7.2 416.1 %copy-start = (s32[8,12]{1,0:T(8,128)S(1)}, s32[8,12]{1,0:T(8,128)}, u32[]{:S(2)}) copy-start(s32[8,12]{1,0:T(8,128)} %param.11) | copy-start | bytes 1156
  7.2 6.4 %copy-start.3 = (f32[256,1024]{1,0:T(8,128)S(1)}, f32[256,1024]{1,0:T(8,128)}, u32[]{:S(2)}) copy-start(f32[256,1024]{1,0:T(8,128)} %param.7) | copy-start | bytes 3145732
  7.2 8.0 %copy-start.2 = (bf16[2,256,1024]{2,1,0:T(8,128)(2,1)S(1)}, bf16[2,256,1024]{2,1,0:T(8,128)(2,1)}, u32[]{:S(2)}) copy-start(bf16[2,256,1024]{2,1,0:T(8,128)(2,1)} %param.8) | copy-start | bytes 3145732
  7.2 7.7 %copy-start.5 = (s32[8,12]{1,0:T(8,128)S(1)}, s32[8,12]{1,0:T(8,128)}, u32[]{:S(2)}) copy-start(s32[8,12]{1,0:T(8,128)} %param.10) | copy-start | bytes 1156
  7.2 45.1 %all-gather.3.cloned.1.call-start = ((), (), s32[]{:S(2)}) async-start(), calls=%async_computation.1 | async-start | bytes 5242880 | tf_op jit(solution)/shard_map/all_gather | solution.py:23
  62.0 1.9 copy-start.1
  380.0 6.0 copy-start.4
  414.5 99.2 %all-to-all-start = ((bf16[8,256,1024]{2,1,0:T(8,128)(2,1)}), bf16[8,256,1024]{2,1,0:T(8,128)(2,1)}, u32[]{:S(2)}, u32[]{:S(2)}) async-start(bf16[8,256,1024]{2,1,0:T(8,128)(2,1)} %copy.16), calls=%async_computation | async-start | bytes 8388608 | tf_op jit(solution)/shard_map/all_to_all | solution.py:42
  420.1 37.9 %all-gather.5.cloned.1.call-start = ((), (), s32[]{:S(2)}) async-start(), calls=%async_computation.2 | async-start | bytes 5242880 | tf_op jit(solution)/shard_map/all_gather | solution.py:29
Sparse Core Ops, SparseCore 0:
  15.0 37.1 all-gather.2
  423.0 34.9 all-gather.4
where the time goes:
time: 649 us; the launch traced here: 636 us
  other arithmetic  263 us (41%)
  waiting for transfers between devices  127 us (20%)
  matrix products  89.7 us (14%)
  local copies, waits for them, and re-layouts  81.8 us (13%)
  loops' own time  49.3 us (8%)
  between operations  19.6 us (3%)
    another operation x30, other arithmetic, local(): factor = jnp.linalg.cholesky(diag_full)  172 us
    another operation x3, other arithmetic, local(): lax.linalg.triangular_solve(factor, stacked.T, left_side=True, lower=True)  85 us
    all_to_all x1, waiting for transfers between devices, local(): lax.all_to_all(outgoing, 'col', split_axis=0, concat_axis=0, tiled=True)  55.8 us
    another operation x1, loops' own time, local(): buffer = lax.fori_loop(0, own_count, own_step, trailing[0])  49.2 us
    dot_general x12, matrix products, slot_product(): lax.dot_general(left_slice, right_tile, (((1,), (1,)), ((), ())), preferr...  39.8 us
    all_gather x1, waiting for transfers between devices, local(): diag_full = lax.all_gather(diag_block, 'row', axis=0, tiled=True)  36.7 us
    all_gather x1, waiting for transfers between devices, local(): whole_tiles = lax.all_gather(panel_factor, 'row', axis=1, tiled=True)  34.7 us
    another operation x24, local copies, waits for them, and re-layouts  27.8 us
  transfers between devices with their start and end apart: 3, of which 3 were waited for; matrix products, arithmetic and copies ran while one was open for 1% of the time, Pallas kernels for 0%

commit v1 on v0

v1 whole, which is shorter than its diff:
```python
import functools
import jax
import jax.numpy as jnp
from jax import lax
from jax.experimental import pallas as pl
from jax.experimental.pallas import tpu as pltpu
from jax.sharding import PartitionSpec as P

BLOCK = 128
GROUP = 4
SUB = 8
LIMIT = 60 << 20


def split(x):
    high = x.astype(jnp.bfloat16)
    return high, (x - high.astype(jnp.float32)).astype(jnp.bfloat16)


def dot3(ah, al, bh, bl, dims):
    d = functools.partial(
        lax.dot_general, dimension_numbers=(dims, ((), ())), preferred_element_type=jnp.float32
    )
    return d(ah, bh) + (d(ah, bl) + d(al, bh))


def invert_factor(rows):
    rows = list(rows)
    lane = lax.broadcasted_iota(jnp.int32, (SUB, BLOCK), 1)
    sub = lax.broadcasted_iota(jnp.int32, (SUB, BLOCK), 0)
    lane1 = lane[:1]
    for c in range(0, BLOCK, GROUP):
        v0, s = divmod(c, SUB)
        last = s + GROUP == SUB
        strips = range(v0, len(rows))
        cols = [
            {i: jnp.broadcast_to(rows[i][:, c + j : c + j + 1], (SUB, BLOCK)) for i in strips}
            for j in range(GROUP)
        ]
        piv = [[cols[j][v0][s + i : s + i + 1, :] for j in range(i + 1)] for i in range(GROUP)]
        low = [[None] * GROUP for _ in range(GROUP)]
        inv = []
        for t in range(GROUP):
            for i in range(t, GROUP):
                low[i][t] = piv[i][t]
            for m in range(t):
                for i in range(t, GROUP):
                    low[i][t] = low[i][t] - low[i][m] * low[t][m]
            inv.append(lax.rsqrt(low[t][t]))
            for i in range(t + 1, GROUP):
                low[i][t] = low[i][t] * inv[t]
        ingroup1 = (lane1 >= c) & (lane1 < c + GROUP)
        solved = []
        for t in range(GROUP):
            x = rows[v0][s + t : s + t + 1, :]
            x = jnp.where(ingroup1, jnp.where(lane1 == c + t, 1.0, 0.0), x)
            for m in range(t):
                x = x - low[t][m] * solved[m]
            solved.append(x * inv[t])
        wide = [jnp.broadcast_to(x, (SUB, BLOCK)) for x in solved]
        ingroup = (lane >= c) & (lane < c + GROUP)
        for i in strips:
            if i == v0 and last:
                new = rows[i]
            else:
                mult = []
                new = jnp.where(ingroup, 0.0, rows[i])
                for t in range(GROUP):
                    y = cols[t][i]
                    for m in range(t):
                        y = y - mult[m] * low[t][m]
                    mult.append(y * inv[t])
                    new = new - mult[t] * wide[t]
            if i == v0:
                if not last:
                    new = jnp.where(sub >= s + GROUP, new, rows[i])
                for t in range(GROUP):
                    new = jnp.where(sub == s + t, wide[t], new)
            rows[i] = new
    return rows


def factor_kernel(diag_ref, high_ref, low_ref, work, row_high, row_low):
    n = diag_ref.shape[0]
    steps = n // BLOCK
    work[...] = diag_ref[...]
    row_id = lax.broadcasted_iota(jnp.int32, (BLOCK, BLOCK), 0)
    lane_id = lax.broadcasted_iota(jnp.int32, (BLOCK, BLOCK), 1)

    @pl.loop(0, steps)
    def _(k):
        here = pl.multiple_of(k * BLOCK, BLOCK)
        strips = [
            work[pl.ds(pl.multiple_of(here + i * SUB, SUB), SUB), pl.ds(here, BLOCK)]
            for i in range(BLOCK // SUB)
        ]
        inverse = jnp.concatenate(invert_factor(strips), axis=0)
        inverse = jnp.where(lane_id <= row_id, inverse, 0.0)
        ih, il = split(inverse)
        xh, xl = split(work[pl.ds(here, BLOCK), :])
        panel = dot3(ih, il, xh, xl, ((1,), (0,)))
        ph, plow = split(panel)
        work[pl.ds(here, BLOCK), :] = panel
        row_high[...] = ph
        row_low[...] = plow
        work[pl.ds(here, BLOCK), pl.ds(here, BLOCK)] = inverse
        row_high[:, pl.ds(here, BLOCK)] = ih
        row_low[:, pl.ds(here, BLOCK)] = il

        @pl.loop(k + 1, steps)
        def _(i):
            there = pl.multiple_of(i * BLOCK, BLOCK)
            lh = row_high[:, pl.ds(there, BLOCK)]
            ll = row_low[:, pl.ds(there, BLOCK)]
            work[pl.ds(there, BLOCK), pl.ds(here, BLOCK)] = jnp.zeros((BLOCK, BLOCK), jnp.float32)
            work[pl.ds(there, BLOCK), :] -= dot3(
                lh, ll, row_high[...], row_low[...], ((0,), (0,))
            )

    @pl.loop(0, steps)
    def _(k):
        here = pl.multiple_of(k * BLOCK, BLOCK)
        strip = work[pl.ds(here, BLOCK), :]
        r = lax.broadcasted_iota(jnp.int32, strip.shape, 0) + here
        c = lax.broadcasted_iota(jnp.int32, strip.shape, 1)
        h, l = split(jnp.where(c <= r, strip, 0.0))
        high_ref[pl.ds(here, BLOCK), :] = h
        low_ref[pl.ds(here, BLOCK), :] = l


def invert(diag):
    n = diag.shape[0]
    vmem = pl.BlockSpec(memory_space=pltpu.VMEM)
    return pl.pallas_call(
        factor_kernel,
        out_shape=[jax.ShapeDtypeStruct((n, n), jnp.bfloat16)] * 2,
        in_specs=[vmem],
        out_specs=[vmem, vmem],
        scratch_shapes=[
            pltpu.VMEM((n, n), jnp.float32),
            pltpu.VMEM((BLOCK, n), jnp.bfloat16),
            pltpu.VMEM((BLOCK, n), jnp.bfloat16),
        ],
        compiler_params=pltpu.CompilerParams(vmem_limit_bytes=LIMIT),
        cost_estimate=pl.CostEstimate(
            flops=60 * n**3, bytes_accessed=8 * n * n, transcendentals=n
        ),
        name="invert_factor",
    )(diag)


def solve_kernel(x_ref, high_ref, low_ref, out_ref):
    dims = (((1,), (1,)), ((), ()))
    x = x_ref[...]
    y = lax.dot_general(x, low_ref[...], dims, preferred_element_type=jnp.float32)
    y = y + lax.dot_general(x, high_ref[...], dims, preferred_element_type=jnp.float32)
    out_ref[...] = y.astype(out_ref.dtype)


def solve(x, high, low):
    m, n = x.shape
    rows = min(256, m)
    resident = pl.BlockSpec((n, n), lambda i: (0, 0), pipeline_mode=pl.Buffered(1))
    block = pl.BlockSpec((rows, n), lambda i: (i, 0))
    return pl.pallas_call(
        solve_kernel,
        grid=(m // rows,),
        out_shape=jax.ShapeDtypeStruct((m, n), jnp.bfloat16),
        in_specs=[block, resident, resident],
        out_specs=block,
        compiler_params=pltpu.CompilerParams(vmem_limit_bytes=LIMIT),
        name="solve_rows",
    )(x, high, low)


def slot_kernel(live_ref, left_id_ref, col_id_ref, left_ref, right_ref, trail_ref, out_ref):
    s = pl.program_id(0)

    @pl.when(live_ref[s] > 0)
    def _():
        product = lax.dot_general(
            left_ref[...],
            right_ref[...],
            (((1,), (1,)), ((), ())),
            preferred_element_type=jnp.float32,
        )
        out_ref[...] = (trail_ref[...].astype(jnp.float32) - product).astype(out_ref.dtype)

    @pl.when(live_ref[s] == 0)
    def _():
        out_ref[...] = trail_ref[...]


def apply_slots(live, left_ids, col_ids, slices, tiles, trailing):
    slots, rows, n = trailing.shape
    return pl.pallas_call(
        slot_kernel,
        out_shape=jax.ShapeDtypeStruct(trailing.shape, trailing.dtype),
        grid_spec=pltpu.PrefetchScalarGridSpec(
            num_scalar_prefetch=3,
            grid=(slots,),
            in_specs=[
                pl.BlockSpec((None, rows, n), lambda s, v, a, b: (a[s], 0, 0)),
                pl.BlockSpec((None, n, n), lambda s, v, a, b: (b[s], 0, 0)),
                pl.BlockSpec((None, rows, n), lambda s, v, a, b: (s, 0, 0)),
            ],
            out_specs=pl.BlockSpec((None, rows, n), lambda s, v, a, b: (s, 0, 0)),
        ),
        compiler_params=pltpu.CompilerParams(vmem_limit_bytes=LIMIT),
        name="apply_slots",
    )(live, left_ids, col_ids, slices, tiles, trailing)


def local(diag_block, panel, trailing, slot_rows, slot_cols):
    tile_count, row_count, n = panel.shape
    diag_full = lax.all_gather(diag_block, "row", axis=0, tiled=True)
    column_index = lax.axis_index("col")
    own_rows = lax.dynamic_index_in_dim(slot_rows, column_index, 0, keepdims=False)
    own_cols = lax.dynamic_index_in_dim(slot_cols, column_index, 0, keepdims=False)
    mine = (slot_rows >= 0) & (slot_rows // tile_count == column_index)
    local_pick = jnp.max(jnp.where(mine, slot_rows % tile_count, 0), axis=1)
    outgoing = jnp.broadcast_to(panel[0], (slot_rows.shape[0], row_count, n))
    for p in range(1, tile_count):
        outgoing = jnp.where((local_pick == p)[:, None, None], panel[p], outgoing)
    raw_slices = lax.all_to_all(outgoing, "col", split_axis=0, concat_axis=0, tiled=True)
    raw_tiles = lax.all_gather(panel, "row", axis=1, tiled=True)
    high, low = invert(diag_full)
    tiles = solve(raw_tiles.reshape(-1, n), high, low).reshape(raw_tiles.shape)
    slices = solve(raw_slices.reshape(-1, n), high, low).reshape(raw_slices.shape)
    panel_factor = lax.dynamic_slice_in_dim(
        tiles, lax.axis_index("row") * row_count, row_count, axis=1
    )
    live = (own_rows >= 0).astype(jnp.int32)
    left_ids = jnp.maximum(own_rows, 0) // tile_count
    updated = apply_slots(live, left_ids, own_cols, slices, tiles, trailing[0])
    return (panel_factor, updated[None])


def solution(mesh):
    return jax.shard_map(
        local,
        mesh=mesh,
        in_specs=(P("row", None), P("col", "row", None), P("col", None, "row", None), P(), P()),
        out_specs=(P("col", "row", None), P("col", None, "row", None)),
        check_vma=False,
    )
```

time: 649 us -> 156 us (0.24); the launches traced: 636 us -> 154 us
  other arithmetic: 263 us -> 5.77 us
  waiting for transfers between devices: 127 us -> 24.6 us
  Pallas kernels: 0 us -> 98.5 us
  matrix products: 89.7 us -> 0 us
  local copies, waits for them, and re-layouts: 81.8 us -> 4.11 us
  loops' own time: 49.3 us -> 0 us
    another operation x33 -> x0, other arithmetic: 257 us -> none  [the longest x30 172 us: local(): factor = jnp.linalg.cholesky(diag_full)]
    pallas_call x0 -> x4, Pallas kernels: none -> 98.5 us  [the longest x1 53.8 us: invert(): pl.pallas_call(factor_kernel, out_shape=[jax.ShapeDtypeStruct((n, n), jnp...]
    all_to_all x1, waiting for transfers between devices: 55.8 us -> 0.01 us  [local(): lax.all_to_all(outgoing, 'col', split_axis=0, concat_axis=0, tiled=True)]
    another operation x2 -> x0, loops' own time: 49.3 us -> none  [the longest x1 49.2 us: local(): buffer = lax.fori_loop(0, own_count, own_step, trailing[0])]
    another operation x29 -> x0, matrix products: 48.1 us -> none  [the longest x15 25 us: local(): lax.linalg.triangular_solve(factor, stacked.T, left_side=True, lower=True)]
    dot_general x13 -> x0, matrix products: 41.6 us -> none  [the longest x12 39.8 us: slot_product(): lax.dot_general(left_slice, right_tile, (((1,), (1,)), ((), ())), preferr...]
    all_gather x1, waiting for transfers between devices: 34.7 us -> 0.01 us  [local(): raw_tiles = lax.all_gather(panel, 'row', axis=1, tiled=True)]
    another operation x34 -> x0, local copies, waits for them, and re-layouts: 30.3 us -> none
  transfers between devices with their start and end apart: 3 -> 3, of which waited for: 3 -> 1; matrix products, arithmetic and copies ran while one was open for 1% -> 6% of each run, Pallas kernels for 0% -> 44%
where the time goes in v1:
time: 156 us; the launch traced here: 154 us
  Pallas kernels  98.5 us (63%)
  waiting for transfers between devices  24.6 us (16%)
  between operations  14.1 us (9%)
  starting transfers between devices  7.36 us (5%)
  other arithmetic  5.77 us (4%)
  local copies, waits for them, and re-layouts  4.11 us (3%)
    pallas_call x1, Pallas kernels, invert(): pl.pallas_call(factor_kernel, out_shape=[jax.ShapeDtypeStruct((n, n), jnp...  53.8 us
    pallas_call x2, Pallas kernels, solve(): pl.pallas_call(solve_kernel, grid=(m // rows,), out_shape=jax.ShapeDtypeS...  27.3 us
    all_gather x1, waiting for transfers between devices, local(): diag_full = lax.all_gather(diag_block, 'row', axis=0, tiled=True)  23.2 us
    pallas_call x1, Pallas kernels, apply_slots(): pl.pallas_call(slot_kernel, out_shape=jax.ShapeDtypeStruct(trailing.shape...  17.4 us
    all_to_all x1, starting transfers between devices, local(): lax.all_to_all(outgoing, 'col', split_axis=0, concat_axis=0, tiled=True)  7.28 us
  transfers between devices with their start and end apart: 3, of which 1 were waited for; matrix products, arithmetic and copies ran while one was open for 6% of the time, Pallas kernels for 44%

profile of v1, /device:TPU:0, one launch (start us, length us, event | category | flops | bytes accessed | tf_op | source)
XLA Modules:
  0.0 154.4 jit_solution(6521968103583492979)
XLA Ops:
  7.2 0.0 copy-start
  7.2 0.0 all-gather.5.cloned.1.call-start
  7.2 0.7 all-gather.5.cloned.1.call-update
  7.9 0.8 fusion.2
  8.7 1.3 slice_bitcast_fusion.1
  10.0 2.5 %broadcast_select_fusion = bf16[8,256,1024]{2,1,0:T(8,128)(2,1)} fusion(pred[8]{0:T(512)(128)(4,1)S(1)} %broadcast_compare_fusion, bf16[256,1024]{1,0:T(8,128)(2,1)S(1)} %get-tuple-element.7, bf16[256,1024]{1,0:T(8,128)(2,1)S(1)} %get-tuple-element.6), kind=kLoop, calls=%fused_computation | loop fusion | flops 2097152 | bytes 5242888 | tf_op jit(solution)/shard_map/jit(_where)/select_n | solution.py:224
  12.6 7.3 %all-to-all-start = ((bf16[8,256,1024]{2,1,0:T(8,128)(2,1)}), bf16[8,256,1024]{2,1,0:T(8,128)(2,1)}, u32[]{:S(2)}, u32[]{:S(2)}) async-start(bf16[8,256,1024]{2,1,0:T(8,128)(2,1)} %broadcast_select_fusion), calls=%async_computation | async-start | bytes 8388608 | tf_op jit(solution)/shard_map/all_to_all | solution.py:225
  19.8 0.0 all-gather.3.cloned.1.call-start
  19.9 0.7 all-gather.3.cloned.1.call-update
  20.6 1.2 bitcast_select_fusion.left_id_ref
  21.8 1.2 fusion.5.live_ref
  23.0 0.0 copy-done
  23.0 0.6 fusion.4.col_id_ref
  23.6 23.2 %all-gather.5.cloned.1.call-done.diag_ref = f32[1024,1024]{1,0:T(8,128)} async-done(((f32[256,1024]{1,0:T(8,128)}), f32[1024,1024]{1,0:T(8,128)}) %all-gather.5.cloned.1.call-update) | async-done | bytes 4194320 | tf_op jit(solution)/shard_map/all_gather | solution.py:216
  46.8 53.8 %invert_factor.1 = (bf16[1024,1024]{1,0:T(8,128)(2,1)}, bf16[1024,1024]{1,0:T(8,128)(2,1)}) custom-call(f32[1024,1024]{1,0:T(8,128)} %all-gather.5.cloned.1.call-done.diag_ref), custom_call_target="tpu_custom_call" | custom-call | flops 64424509440 | bytes 8388608 | tf_op jit(solution)/shard_map/invert_factor/pallas_call | solution.py:134
  100.6 0.0 all-gather.3.cloned.1.call-done
  100.6 13.7 %solve_rows.2 = bf16[2048,1024]{1,0:T(8,128)(2,1)} custom-call(bf16[2048,1024]{1,0:T(8,128)(2,1)} %bitcast.23, bf16[1024,1024]{1,0:T(8,128)(2,1)} %get-tuple-element.4.high_ref, bf16[1024,1024]{1,0:T(8,128)(2,1)} %get-tuple-element.5.low_ref), custom_call_target="tpu_custom_call" | custom-call | tf_op jit(solution)/shard_map/solve_rows/pallas_call | solution.py:165
  114.3 2.3 %constant_dynamic-slice_fusion.2 = bf16[2,256,1024]{2,1,0:T(8,128)(2,1)} fusion(bf16[2,1024,1024]{2,1,0:T(8,128)(2,1)} %bitcast.18, s32[]{:T(128)S(6)} %select_n.33), kind=kLoop, calls=%fused_computation.17 | loop fusion | bytes 2097156 | tf_op jit(solution)/shard_map/dynamic_slice | solution.py:230
  116.5 0.0 all-to-all-done
  116.5 13.6 %solve_rows.3 = bf16[2048,1024]{1,0:T(8,128)(2,1)} custom-call(bf16[2048,1024]{1,0:T(8,128)(2,1)} %bitcast.8.x_ref, bf16[1024,1024]{1,0:T(8,128)(2,1)} %get-tuple-element.4.high_ref, bf16[1024,1024]{1,0:T(8,128)(2,1)} %get-tuple-element.5.low_ref), custom_call_target="tpu_custom_call" | custom-call | tf_op jit(solution)/shard_map/solve_rows/pallas_call | solution.py:165
  130.1 17.4 %apply_slots.1 = bf16[12,256,1024]{2,1,0:T(8,128)(2,1)} custom-call(s32[12]{0:T(128)} %fusion.5.live_ref, s32[12]{0:T(128)} %bitcast_select_fusion.left_id_ref, s32[12]{0:T(128)} %fusion.4.col_id_ref, bf16[8,256,1024]{2,1,0:T(8,128)(2,1)} %bitcast.20, bf16[2,1024,1024]{2,1,0:T(8,128)(2,1)} %bitcast.19, bf16[12,256,1024]{2,1,0:T(8,128)(2,1)} %bitcast.21), custom_call_target="tpu_custom_call" | custom-call | tf_op jit(solution)/shard_map/apply_slots/pallas_call | solution.py:196
  (1 shorter events, 0.0 us)
Async XLA Ops:
  7.2 15.8 %copy-start = (s32[8,12]{1,0:T(8,128)S(1)}, s32[8,12]{1,0:T(8,128)}, u32[]{:S(2)}) copy-start(s32[8,12]{1,0:T(8,128)} %param.9) | copy-start | bytes 1156
  7.2 39.6 %all-gather.5.cloned.1.call-start = ((), (), s32[]{:S(2)}) async-start(), calls=%async_computation.2 | async-start | bytes 5242880 | tf_op jit(solution)/shard_map/all_gather | solution.py:216
  12.6 104.0 %all-to-all-start = ((bf16[8,256,1024]{2,1,0:T(8,128)(2,1)}), bf16[8,256,1024]{2,1,0:T(8,128)(2,1)}, u32[]{:S(2)}, u32[]{:S(2)}) async-start(bf16[8,256,1024]{2,1,0:T(8,128)(2,1)} %broadcast_select_fusion), calls=%async_computation | async-start | bytes 8388608 | tf_op jit(solution)/shard_map/all_to_all | solution.py:225
  19.8 80.8 %all-gather.3.cloned.1.call-start = ((), (), s32[]{:S(2)}) async-start(), calls=%async_computation.1 | async-start | bytes 5242880 | tf_op jit(solution)/shard_map/all_gather | solution.py:226
Sparse Core Ops, SparseCore 0:
  9.5 37.1 all-gather.4
  48.3 34.4 all-gather.2

commit v2 on v1

--- a/solution.py
+++ b/solution.py
@@ -10,6 +10,9 @@
 GROUP = 4
 SUB = 8
 LIMIT = 60 << 20
+WIDE = 256
+CHUNK = 1024
+OWNED = 1024
 
 
 def split(x):
@@ -149,66 +152,128 @@
     )(diag)
 
 
-def solve_kernel(x_ref, high_ref, low_ref, out_ref):
+def solve_into(x, high_ref, low_ref, store):
+    n = x.shape[1]
     dims = (((1,), (1,)), ((), ()))
-    x = x_ref[...]
-    y = lax.dot_general(x, low_ref[...], dims, preferred_element_type=jnp.float32)
-    y = y + lax.dot_general(x, high_ref[...], dims, preferred_element_type=jnp.float32)
-    out_ref[...] = y.astype(out_ref.dtype)
-
-
-def solve(x, high, low):
-    m, n = x.shape
-    rows = min(256, m)
-    resident = pl.BlockSpec((n, n), lambda i: (0, 0), pipeline_mode=pl.Buffered(1))
-    block = pl.BlockSpec((rows, n), lambda i: (i, 0))
+    for j in range(0, n, WIDE):
+        end = min(j + WIDE, n)
+        y = lax.dot_general(
+            x[:, :end], low_ref[j:end, :end], dims, preferred_element_type=jnp.float32
+        ) + lax.dot_general(
+            x[:, :end], high_ref[j:end, :end], dims, preferred_element_type=jnp.float32
+        )
+        store(slice(j, end), y.astype(jnp.bfloat16))
+
+
+def finish_kernel(
+    plan, place_ref, live_ref, left_id_ref, col_id_ref, wanted_ref,
+    high_ref, low_ref, tile_ref, slice_ref, trail_ref,
+    factor_ref, out_ref, tiles, slices,
+):
+    chunks, per_tile, chunk, owner_steps, owners = plan
+    step = pl.program_id(0)
+    row_count = factor_ref.shape[1]
+
+    @pl.when(step < chunks)
+    def _():
+        tile = step // per_tile
+        start = pl.multiple_of((step % per_tile) * chunk, chunk)
+
+        def store(cols, y):
+            tiles[tile, pl.ds(start, chunk), cols] = y
+
+        solve_into(tile_ref[...], high_ref, low_ref, store)
+
+    @pl.when((step >= chunks) & (step < chunks + owner_steps))
+    def _():
+        first = (step - chunks) * owners
+        need = wanted_ref[first]
+        for q in range(1, owners):
+            need = need + wanted_ref[first + q]
+
+        @pl.when(need > 0)
+        def _():
+            def store(cols, y):
+                slices[pl.ds(first, owners), :, cols] = y.reshape(owners, row_count, -1)
+
+            x = slice_ref[...].reshape(owners * row_count, -1)
+            solve_into(x, high_ref, low_ref, store)
+
+    @pl.when(step == chunks)
+    def _():
+        start = pl.multiple_of(place_ref[0] * row_count, row_count)
+        factor_ref[...] = tiles[:, pl.ds(start, row_count), :]
+
+    @pl.when(step >= chunks + owner_steps)
+    def _():
+        s = step - chunks - owner_steps
+
+        @pl.when(live_ref[s] > 0)
+        def _():
+            product = lax.dot_general(
+                slices[left_id_ref[s]],
+                tiles[col_id_ref[s]],
+                (((1,), (1,)), ((), ())),
+                preferred_element_type=jnp.float32,
+            )
+            out_ref[...] = (trail_ref[...].astype(jnp.float32) - product).astype(out_ref.dtype)
+
+        @pl.when(live_ref[s] == 0)
+        def _():
+            out_ref[...] = trail_ref[...]
+
+
+def finish(place, live, left_ids, col_ids, wanted, high, low, raw_tiles, raw_slices, trailing):
+    slots, row_count, n = trailing.shape
+    tile_count = raw_tiles.shape[0]
+    col_count = raw_slices.shape[0]
+    chunk = min(CHUNK, n)
+    per_tile = n // chunk
+    chunks = tile_count * per_tile
+    owners = max(1, min(col_count, OWNED // row_count))
+    owner_steps = col_count // owners
+    plan = (chunks, per_tile, chunk, owner_steps, owners)
+    before = chunks + owner_steps
+    resident = pl.BlockSpec((n, n), lambda i, *_: (0, 0), pipeline_mode=pl.Buffered(1))
+
+    def tile_map(i, *_):
+        i = jnp.minimum(i, chunks - 1)
+        return (i // per_tile, i % per_tile, 0)
+
+    def slice_map(i, *_):
+        return (jnp.clip(i - chunks, 0, owner_steps - 1), 0, 0)
+
+    def slot_map(i, *_):
+        return (jnp.clip(i - before, 0, slots - 1), 0, 0)
+
     return pl.pallas_call(
-        solve_kernel,
-        grid=(m // rows,),
-        out_shape=jax.ShapeDtypeStruct((m, n), jnp.bfloat16),
-        in_specs=[block, resident, resident],
-        out_specs=block,
-        compiler_params=pltpu.CompilerParams(vmem_limit_bytes=LIMIT),
-        name="solve_rows",
-    )(x, high, low)
-
-
-def slot_kernel(live_ref, left_id_ref, col_id_ref, left_ref, right_ref, trail_ref, out_ref):
-    s = pl.program_id(0)
-
-    @pl.when(live_ref[s] > 0)
-    def _():
-        product = lax.dot_general(
-            left_ref[...],
-            right_ref[...],
-            (((1,), (1,)), ((), ())),
-            preferred_element_type=jnp.float32,
-        )
-        out_ref[...] = (trail_ref[...].astype(jnp.float32) - product).astype(out_ref.dtype)
-
-    @pl.when(live_ref[s] == 0)
-    def _():
-        out_ref[...] = trail_ref[...]
-
-
-def apply_slots(live, left_ids, col_ids, slices, tiles, trailing):
-    slots, rows, n = trailing.shape
-    return pl.pallas_call(
-        slot_kernel,
-        out_shape=jax.ShapeDtypeStruct(trailing.shape, trailing.dtype),
+        functools.partial(finish_kernel, plan),
+        out_shape=[
+            jax.ShapeDtypeStruct((tile_count, row_count, n), jnp.bfloat16),
+            jax.ShapeDtypeStruct(trailing.shape, trailing.dtype),
+        ],
         grid_spec=pltpu.PrefetchScalarGridSpec(
-            num_scalar_prefetch=3,
-            grid=(slots,),
+            num_scalar_prefetch=5,
+            grid=(before + slots,),
             in_specs=[
-                pl.BlockSpec((None, rows, n), lambda s, v, a, b: (a[s], 0, 0)),
-                pl.BlockSpec((None, n, n), lambda s, v, a, b: (b[s], 0, 0)),
-                pl.BlockSpec((None, rows, n), lambda s, v, a, b: (s, 0, 0)),
+                resident,
+                resident,
+                pl.BlockSpec((None, chunk, n), tile_map),
+                pl.BlockSpec((owners, row_count, n), slice_map),
+                pl.BlockSpec((None, row_count, n), slot_map),
             ],
-            out_specs=pl.BlockSpec((None, rows, n), lambda s, v, a, b: (s, 0, 0)),
+            out_specs=[
+                pl.BlockSpec((tile_count, row_count, n), lambda i, *_: (0, 0, 0)),
+                pl.BlockSpec((None, row_count, n), slot_map),
+            ],
+            scratch_shapes=[
+                pltpu.VMEM((tile_count, n, n), jnp.bfloat16),
+                pltpu.VMEM((col_count, row_count, n), jnp.bfloat16),
+            ],
         ),
         compiler_params=pltpu.CompilerParams(vmem_limit_bytes=LIMIT),
-        name="apply_slots",
-    )(live, left_ids, col_ids, slices, tiles, trailing)
+        name="finish",
+    )(place, live, left_ids, col_ids, wanted, high, low, raw_tiles, raw_slices, trailing)
 
 
 def local(diag_block, panel, trailing, slot_rows, slot_cols):
@@ -225,14 +290,15 @@
     raw_slices = lax.all_to_all(outgoing, "col", split_axis=0, concat_axis=0, tiled=True)
     raw_tiles = lax.all_gather(panel, "row", axis=1, tiled=True)
     high, low = invert(diag_full)
-    tiles = solve(raw_tiles.reshape(-1, n), high, low).reshape(raw_tiles.shape)
-    slices = solve(raw_slices.reshape(-1, n), high, low).reshape(raw_slices.shape)
-    panel_factor = lax.dynamic_slice_in_dim(
-        tiles, lax.axis_index("row") * row_count, row_count, axis=1
-    )
     live = (own_rows >= 0).astype(jnp.int32)
     left_ids = jnp.maximum(own_rows, 0) // tile_count
-    updated = apply_slots(live, left_ids, own_cols, slices, tiles, trailing[0])
+    owner = jnp.arange(slot_rows.shape[0], dtype=jnp.int32)
+    wanted = jnp.any((left_ids[None, :] == owner[:, None]) & (own_rows >= 0)[None, :], axis=1)
+    place = lax.axis_index("row").astype(jnp.int32).reshape(1)
+    panel_factor, updated = finish(
+        place, live, left_ids, own_cols, wanted.astype(jnp.int32),
+        high, low, raw_tiles, raw_slices, trailing[0],
+    )
     return (panel_factor, updated[None])
 
 

time: 156 us -> 150 us (0.962)
  Pallas kernels: 98.5 us -> 83.3 us
  waiting for transfers between devices: 24.6 us -> 37.1 us
  local copies, waits for them, and re-layouts: 4.11 us -> 1.85 us
    pallas_call x3 -> x1, Pallas kernels: 44.7 us -> 29.5 us  [finish(): pl.pallas_call(functools.partial(finish_kernel, plan), out_shape=[jax.Sha...]
    all_to_all x1, waiting for transfers between devices: 0.01 us -> 12.5 us  [local(): lax.all_to_all(outgoing, 'col', split_axis=0, concat_axis=0, tiled=True)]
    dynamic_slice x1 -> x0, local copies, waits for them, and re-layouts: 2.26 us -> none  [local(): lax.dynamic_slice_in_dim(tiles, lax.axis_index('row') * row_count, row_co...]
  transfers between devices with their start and end apart: 3 -> 3, of which waited for: 1 -> 2; matrix products, arithmetic and copies ran while one was open for 6% -> 5% of each run, Pallas kernels for 44% -> 36%
where the time goes in v2:
time: 150 us; the launch traced here: 149 us
  Pallas kernels  83.3 us (56%)
  waiting for transfers between devices  37.1 us (25%)
  between operations  14.1 us (9%)
  starting transfers between devices  7.36 us (5%)
  other arithmetic  5.75 us (4%)
  local copies, waits for them, and re-layouts  1.85 us (1%)
    pallas_call x1, Pallas kernels, invert(): pl.pallas_call(factor_kernel, out_shape=[jax.ShapeDtypeStruct((n, n), jnp...  53.8 us
    pallas_call x1, Pallas kernels, finish(): pl.pallas_call(functools.partial(finish_kernel, plan), out_shape=[jax.Sha...  29.5 us
    all_gather x1, waiting for transfers between devices, local(): diag_full = lax.all_gather(diag_block, 'row', axis=0, tiled=True)  23.2 us
    all_to_all x1, waiting for transfers between devices, local(): lax.all_to_all(outgoing, 'col', split_axis=0, concat_axis=0, tiled=True)  12.5 us
    all_to_all x1, starting transfers between devices, local(): lax.all_to_all(outgoing, 'col', split_axis=0, concat_axis=0, tiled=True)  7.28 us
  transfers between devices with their start and end apart: 3, of which 2 were waited for; matrix products, arithmetic and copies ran while one was open for 5% of the time, Pallas kernels for 36%

profile of v2, /device:TPU:0, one launch (start us, length us, event | category | flops | bytes accessed | tf_op | source)
XLA Modules:
  0.0 149.4 jit_solution(10773738934097409284)
XLA Ops:
  7.2 0.0 copy-start
  7.2 0.0 all-gather.3.cloned.1.call-start
  7.2 0.7 all-gather.3.cloned.1.call-update
  7.9 0.8 fusion.2
  8.7 1.3 slice_bitcast_fusion.1
  10.0 2.5 %broadcast_select_fusion = bf16[8,256,1024]{2,1,0:T(8,128)(2,1)} fusion(pred[8]{0:T(512)(128)(4,1)S(1)} %broadcast_compare_fusion, bf16[256,1024]{1,0:T(8,128)(2,1)S(1)} %get-tuple-element.13, bf16[256,1024]{1,0:T(8,128)(2,1)S(1)} %get-tuple-element.12), kind=kLoop, calls=%fused_computation | loop fusion | flops 2097152 | bytes 5242888 | tf_op jit(solution)/shard_map/jit(_where)/select_n | solution.py:289
  12.6 7.3 %all-to-all-start = ((bf16[8,256,1024]{2,1,0:T(8,128)(2,1)}), bf16[8,256,1024]{2,1,0:T(8,128)(2,1)}, u32[]{:S(2)}, u32[]{:S(2)}) async-start(bf16[8,256,1024]{2,1,0:T(8,128)(2,1)} %broadcast_select_fusion), calls=%async_computation | async-start | bytes 8388608 | tf_op jit(solution)/shard_map/all_to_all | solution.py:290
  19.8 0.0 all-gather.5.cloned.1.call-start
  19.9 0.7 all-gather.5.cloned.1.call-update
  20.6 0.7 compare_bitcast_fusion
  21.3 0.1 fusion.4
  21.4 0.5 bitcast_select_fusion.left_id_ref
  22.0 0.0 copy-done
  22.0 0.6 dynamic-slice_bitcast_fusion.col_id_ref
  22.5 0.5 convert_element_type.10.wanted_ref
  23.1 0.5 fusion.7.live_ref
  23.5 23.2 %all-gather.3.cloned.1.call-done.diag_ref = f32[1024,1024]{1,0:T(8,128)} async-done(((f32[256,1024]{1,0:T(8,128)}), f32[1024,1024]{1,0:T(8,128)}) %all-gather.3.cloned.1.call-update) | async-done | bytes 4194320 | tf_op jit(solution)/shard_map/all_gather | solution.py:281
  46.8 53.8 %invert_factor.1 = (bf16[1024,1024]{1,0:T(8,128)(2,1)}, bf16[1024,1024]{1,0:T(8,128)(2,1)}) custom-call(f32[1024,1024]{1,0:T(8,128)} %all-gather.3.cloned.1.call-done.diag_ref), custom_call_target="tpu_custom_call" | custom-call | flops 64424509440 | bytes 8388608 | tf_op jit(solution)/shard_map/invert_factor/pallas_call | solution.py:137
  100.6 0.0 all-gather.5.cloned.1.call-done.tile_ref
  100.6 12.5 %all-to-all-done.slice_ref = bf16[8,256,1024]{2,1,0:T(8,128)(2,1)} async-done(((bf16[8,256,1024]{2,1,0:T(8,128)(2,1)}), bf16[8,256,1024]{2,1,0:T(8,128)(2,1)}, u32[]{:S(2)}, u32[]{:S(2)}) %all-to-all-start) | async-done | bytes 4194336 | tf_op jit(solution)/shard_map/all_to_all | solution.py:290
  113.1 29.5 %finish.1 = (bf16[2,256,1024]{2,1,0:T(8,128)(2,1)}, bf16[12,256,1024]{2,1,0:T(8,128)(2,1)}) custom-call(s32[1]{0:T(128)} %bitcast.place_ref, s32[12]{0:T(128)} %fusion.7.live_ref, s32[12]{0:T(128)} %bitcast_select_fusion.left_id_ref, s32[12]{0:T(128)} %dynamic-slice_bitcast_fusion.col_id_ref, s32[8]{0:T(128)} %convert_element_type.10.wanted_ref, ...), custom_call_target="tpu_custom_call" | custom-call | tf_op jit(solution)/shard_map/finish/pallas_call | solution.py:249
  (2 shorter events, 0.0 us)
Async XLA Ops:
  7.2 14.8 %copy-start = (s32[8,12]{1,0:T(8,128)S(1)}, s32[8,12]{1,0:T(8,128)}, u32[]{:S(2)}) copy-start(s32[8,12]{1,0:T(8,128)} %param.9) | copy-start | bytes 1156
  7.2 39.6 %all-gather.3.cloned.1.call-start = ((), (), s32[]{:S(2)}) async-start(), calls=%async_computation.1 | async-start | bytes 5242880 | tf_op jit(solution)/shard_map/all_gather | solution.py:281
  12.6 100.6 %all-to-all-start = ((bf16[8,256,1024]{2,1,0:T(8,128)(2,1)}), bf16[8,256,1024]{2,1,0:T(8,128)(2,1)}, u32[]{:S(2)}, u32[]{:S(2)}) async-start(bf16[8,256,1024]{2,1,0:T(8,128)(2,1)} %broadcast_select_fusion), calls=%async_computation | async-start | bytes 8388608 | tf_op jit(solution)/shard_map/all_to_all | solution.py:290
  19.8 80.8 %all-gather.5.cloned.1.call-start = ((), (), s32[]{:S(2)}) async-start(), calls=%async_computation.2 | async-start | bytes 5242880 | tf_op jit(solution)/shard_map/all_gather | solution.py:291
Sparse Core Ops, SparseCore 0:
  9.5 37.1 all-gather.2
  48.3 34.4 all-gather.4
